TPU v7x, 32 devices: a whole 2x2x4 slice. The times are simulated.
32 devices in a mesh: dp: 8 (over z, y), mp: 4 (over x, core).
Axes of the slice: x: 2, y: 2, z: 4, core: 2. Of those that a mesh axis runs over, the one named last changes fastest.
Arguments:
- activations: bfloat16 [4, 4096, 5120], P(None, 'dp'), may hold values from -60 to 60
- task_weights: bfloat16 [4, 5120, 512], P(None, 'dp', 'mp'), may hold values from -6 to 6
Outputs:
- merged: float32 [5120, 512], P('dp', 'mp')
All inputs are finite; a program needn't handle non-finite values.
Results may differ from a plain program's by a relative error of at most 0.0015.
Values may be sent and summed in bfloat16 or wider, within the bound.
A program may use at most 128 MiB of HBM per device.

v0:
```python
import jax
import jax.numpy as jnp
from jax import lax
from jax.sharding import PartitionSpec as P

ALPHA = 0.9


def dot(left, right, dims):
    return lax.dot_general(left, right, (dims, ((), ())), preferred_element_type=jnp.float32)


def rounded(array):
    return lax.reduce_precision(array, 8, 7)


def split_pair(array):
    coarse = rounded(array)
    high = coarse.astype(jnp.bfloat16)
    low = (array - coarse).astype(jnp.bfloat16)
    return jnp.concatenate([high, low], axis=1)


def shards(activations, task_weights):
    tasks, tokens, width = activations.shape
    cols = task_weights.shape[2]
    total = tasks * tokens * lax.axis_size("dp")
    bf16, f32 = (jnp.bfloat16, jnp.float32)
    flat = activations.reshape(tasks * tokens, width)
    weights = lax.all_gather(task_weights, "dp", axis=1, tiled=True)
    squares = jnp.sum(jnp.square(activations.astype(f32)), axis=1)
    squares_all = jnp.sum(squares, axis=0)[:, None]
    mean = jnp.mean(weights.astype(f32), axis=0)
    mean_pair = split_pair(mean)
    gaps = []
    for task in range(tasks):
        wide = dot(
            activations[task], jnp.concatenate([weights[task], mean_pair], axis=1), ((1,), (0,))
        )
        outputs = rounded(wide[:, :cols])
        gaps.append(outputs - (wide[:, cols : 2 * cols] + wide[:, 2 * cols :]))
    gap = split_pair(jnp.concatenate(gaps, axis=0))
    diag = sum((squares[t][:, None] * (weights[t].astype(f32) - mean) for t in range(tasks)))
    inner = dot(flat, gap, ((0,), (0,)))
    inner = inner[:, :cols] + inner[:, cols:]
    residual = lax.psum_scatter(
        (ALPHA * inner + (1.0 - ALPHA) * diag) / total, "dp", scatter_dimension=0, tiled=True
    )
    full_bf = lax.all_gather(residual.astype(bf16), "dp", axis=0, tiled=True)
    full = full_bf.astype(f32)
    projected = split_pair(dot(flat, full_bf, ((1,), (0,))))
    inner = dot(flat, projected, ((0,), (0,)))
    inner = inner[:, :cols] + inner[:, cols:]
    image = lax.psum_scatter(
        (ALPHA * inner + (1.0 - ALPHA) * squares_all * full) / total,
        "dp",
        scatter_dimension=0,
        tiled=True,
    )
    image_full = lax.all_gather(image.astype(bf16), "dp", axis=0, tiled=True).astype(f32)
    norm0 = jnp.sum(full * full, axis=0)
    alpha0 = norm0 / jnp.sum(full * image_full, axis=0)
    next_full = full - alpha0 * image_full
    norm1 = jnp.sum(next_full * next_full, axis=0)
    beta = norm1 / norm0
    direction = next_full + beta * full
    direction_bf = direction.astype(bf16)
    direction = direction_bf.astype(f32)
    projected = dot(flat, direction_bf, ((1,), (0,)))
    energy = lax.psum(
        (
            ALPHA * jnp.sum(projected * projected, axis=0)
            + (1.0 - ALPHA) * jnp.sum(squares_all * direction * direction, axis=0)
        )
        / total,
        "dp",
    )
    alpha1 = norm1 / energy
    own_mean = jnp.mean(task_weights.astype(f32), axis=0)
    return own_mean + alpha0 * residual + alpha1 * (residual - alpha0 * image + beta * residual)


def solution(mesh):
    return jax.shard_map(
        shards,
        mesh=mesh,
        in_specs=(P(None, "dp", None), P(None, "dp", "mp")),
        out_specs=P("dp", "mp"),
        check_vma=False,
    )
```

profile of v0, /device:TPU:0, one launch (start us, length us, event | category | flops | bytes accessed | tf_op | source)
XLA Modules:
  0.0 432.0 jit_solution(4052554290245626200)
XLA Ops:
  6.5 2.2 copy.6
  8.8 9.5 %fusion = (f32[5120]{0:T(1024)S(1)}, f32[4,5120]{1,0:T(4,128)S(1)}) fusion(bf16[4,512,5120]{2,1,0:T(8,128)(2,1)} %param.2), kind=kLoop, calls=%fused_computation.1 | loop fusion | flops 41917440 | bytes 21073920 | tf_op jit(solution)/shard_map/reduce_sum | solution.py:32
  18.3 0.7 fusion.62
  18.9 79.0 %all-gather.4.cloned.1.call-done = bf16[4,5120,128]{1,2,0:T(8,128)(2,1)} async-done(((bf16[4,640,128]{1,2,0:T(8,128)(2,1)}), bf16[4,5120,128]{1,2,0:T(8,128)(2,1)}) %all-gather.4.cloned.1.call-update) | async-done | bytes 5242896 | tf_op jit(solution)/shard_map/all_gather | solution.py:30
  97.9 3.8 convert_reduce_fusion
  101.8 0.5 reduce-precision_convert_fusion
  102.3 2.1 slice_bitcast_fusion.3
  104.4 6.9 %fusion.30 = f32[512,384]{0,1:T(8,128)} fusion(bf16[4,512,5120]{2,1,0:T(8,128)(2,1)} %param.2, bf16[5120,128]{0,1:T(8,128)(2,1)S(1)} %get-tuple-element.16, bf16[5120,128]{0,1:T(8,128)(2,1)S(1)} %get-tuple-element.15, bf16[5120,128]{0,1:T(8,128)(2,1)} %get-tuple-element.11), kind=kOutput, calls=%fused_computation.65 | convolution fusion | flops 2025062400 | bytes 9961472 | tf_op jit(solution)/shard_map/dot_general | solution.py:10
  111.3 1.3 slice-done.4
  112.6 4.7 %fusion.33 = f32[512,384]{0,1:T(8,128)} fusion(bf16[4,512,5120]{2,1,0:T(8,128)(2,1)S(1)} %bitcast.65, bf16[5120,128]{0,1:T(8,128)(2,1)S(1)} %get-tuple-element.16, bf16[5120,128]{0,1:T(8,128)(2,1)S(1)} %get-tuple-element.15, bf16[5120,128]{0,1:T(8,128)(2,1)} %get-tuple-element.14), kind=kOutput, calls=%fused_computation.66 | convolution fusion | flops 2025062400 | bytes 9961472 | tf_op jit(solution)/shard_map/dot_general | solution.py:10
  117.2 3.7 fusion.36
  120.9 3.3 fusion.39
  124.2 1.6 fusion.53
  126.0 0.2 reduce-precision_convert_fusion.2
  126.2 7.6 %convolution_bitcast_fusion.1 = f32[5120,256]{0,1:T(8,128)} fusion(bf16[2048,5120]{1,0:T(8,128)(2,1)S(1)} %bitcast.66, bf16[2048,128]{0,1:T(8,128)(2,1)S(1)} %get-tuple-element.20, bf16[2048,128]{0,1:T(8,128)(2,1)S(1)} %get-tuple-element.19), kind=kOutput, calls=%fused_computation.5 | convolution fusion | flops 5370806272 | bytes 27262976 | tf_op jit(solution)/shard_map/dot_general | solution.py:10
  133.8 6.0 %fusion.29 = f32[5120,128]{0,1:T(8,128)} fusion(f32[5120,256]{0,1:T(8,128)} %convolution_bitcast_fusion.1, f32[5120,128]{0,1:T(8,128)S(1)} %convert_reduce_fusion, f32[5120]{0:T(1024)S(1)} %bitcast.68, f32[5120]{0:T(1024)S(1)} %bitcast.69, f32[5120]{0:T(1024)S(1)} %bitcast.70, f32[5120]{0:T(1024)S(1)} %bitcast.67, ...), kind=kLoop, calls=%fused_computation.52 | loop fusion | flops 13762560 | bytes 15810560 | tf_op jit(solution)/shard_map/div | solution.py:47
  139.9 69.6 %reduce-scatter.3.cloned.1.call-done = f32[640,128]{0,1:T(8,128)} async-done(((f32[5120,128]{0,1:T(8,128)}), f32[640,128]{0,1:T(8,128)}) %reduce-scatter.3.cloned.1.call-update) | async-done | bytes 327696 | tf_op jit(solution)/shard_map/reduce_scatter | solution.py:46
  209.4 1.7 convert_element_type.68
  211.2 42.2 %all-gather.6.cloned.1.call-done = bf16[5120,128]{0,1:T(8,128)(2,1)} async-done(((bf16[640,128]{0,1:T(8,128)(2,1)}), bf16[5120,128]{0,1:T(8,128)(2,1)}) %all-gather.6.cloned.1.call-update) | async-done | bytes 1310736 | tf_op jit(solution)/shard_map/all_gather | solution.py:49
  253.4 11.6 %reduce-precision_convert_fusion.1 = (bf16[2048,128]{0,1:T(8,128)(2,1)S(1)}, bf16[2048,128]{0,1:T(8,128)(2,1)S(1)}) fusion(bf16[5120,128]{0,1:T(8,128)(2,1)} %all-gather.6.cloned.1.call-done, bf16[2048,5120]{1,0:T(8,128)(2,1)} %bitcast.61), kind=kOutput, calls=%fused_computation.57 | convolution fusion | flops 2685403136 | bytes 23330816 | tf_op jit(solution)/shard_map/dot_general | solution.py:10
  265.0 10.0 %convolution_bitcast_fusion = f32[5120,256]{0,1:T(8,128)S(1)} fusion(bf16[2048,5120]{1,0:T(8,128)(2,1)} %bitcast.62, bf16[2048,128]{0,1:T(8,128)(2,1)S(1)} %get-tuple-element.18, bf16[2048,128]{0,1:T(8,128)(2,1)S(1)} %get-tuple-element.17), kind=kOutput, calls=%fused_computation.4 | convolution fusion | flops 5370806272 | bytes 27262976 | tf_op jit(solution)/shard_map/dot_general | solution.py:10
  275.0 2.0 fusion.22
  277.1 69.6 %reduce-scatter.5.cloned.1.call-done = f32[640,128]{0,1:T(8,128)} async-done(((f32[5120,128]{0,1:T(8,128)}), f32[640,128]{0,1:T(8,128)}) %reduce-scatter.5.cloned.1.call-update) | async-done | bytes 327696 | tf_op jit(solution)/shard_map/reduce_scatter | solution.py:54
  346.6 1.7 convert_element_type.72
  348.6 41.8 %all-gather.8.cloned.1.call-done = bf16[5120,128]{0,1:T(8,128)(2,1)} async-done(((bf16[640,128]{0,1:T(8,128)(2,1)}), bf16[5120,128]{0,1:T(8,128)(2,1)}) %all-gather.8.cloned.1.call-update) | async-done | bytes 1310736 | tf_op jit(solution)/shard_map/all_gather | solution.py:60
  390.4 2.0 fusion.23
  392.5 0.7 multiply_reduce_fusion
  393.1 1.1 fusion.19
  394.3 11.1 %fusion.42 = f32[128]{0:T(128)S(1)} fusion(bf16[5120,128]{0,1:T(8,128)(2,1)S(1)} %get-tuple-element.10, bf16[2048,5120]{1,0:T(8,128)(2,1)} %bitcast.63), kind=kOutput, calls=%fused_computation.69 | convolution fusion | flops 2684878848 | bytes 22282752 | tf_op jit(solution)/shard_map/dot_general | solution.py:10
  405.4 19.0 %psum.7 = f32[128]{0:T(128)S(1)} all-reduce(f32[128]{0:T(128)S(1)} %add_multiply_fusion), channel_id=1, replica_groups=mesh['dp'=8,'mp'=4] {'dp'}, use_global_device_ids=true, to_apply=%region_11.0 | all-reduce | flops 128 | bytes 1024 | tf_op jit(solution)/shard_map/psum | solution.py:70
  424.4 0.2 multiply_add_fusion
  424.6 0.9 copy.7
  (44 shorter events, 0.8 us)
Async XLA Ops:
  6.5 91.4 %all-gather.4.cloned.1.call-start = ((), (), s32[]{:S(2)}) async-start(), calls=%async_computation.2 | async-start | bytes 5898240 | tf_op jit(solution)/shard_map/all_gather | solution.py:30
  8.8 200.7 %reduce-scatter.3.cloned.1.call-start = ((), (), s32[]{:S(2)}) async-start(), calls=%async_computation.3 | async-start | bytes 2949120 | tf_op jit(solution)/shard_map/reduce_scatter | solution.py:46
  97.9 4.3 copy-start
  101.7 9.5 %slice-start = ((s8[20971520]{0:T(1024)(128)(4,1)}), s8[4194304]{0:T(1024)(128)(4,1)S(1)}, s32[]{:S(2)}) async-start(s8[20971520]{0:T(1024)(128)(4,1)} %bitcast.64), calls=%async_computation.7 | async-start | bytes 8388608
  102.2 9.0 %slice-start.1 = ((s8[20971520]{0:T(1024)(128)(4,1)}), s8[4194304]{0:T(1024)(128)(4,1)S(1)}, s32[]{:S(2)}) async-start(s8[20971520]{0:T(1024)(128)(4,1)} %bitcast.64), calls=%async_computation.8 | async-start | bytes 8388608
  102.3 9.0 %slice-start.2 = ((s8[20971520]{0:T(1024)(128)(4,1)}), s8[4194304]{0:T(1024)(128)(4,1)S(1)}, s32[]{:S(2)}) async-start(s8[20971520]{0:T(1024)(128)(4,1)} %bitcast.64), calls=%async_computation.9 | async-start | bytes 8388608
  104.4 6.9 %slice-start.3 = ((s8[20971520]{0:T(1024)(128)(4,1)}), s8[4194304]{0:T(1024)(128)(4,1)S(1)}, s32[]{:S(2)}) async-start(s8[20971520]{0:T(1024)(128)(4,1)} %bitcast.64), calls=%async_computation.10 | async-start | bytes 8388608
  104.4 8.2 %slice-start.4 = ((s8[20971520]{0:T(1024)(128)(4,1)}), s8[4194304]{0:T(1024)(128)(4,1)S(1)}, s32[]{:S(2)}) async-start(s8[20971520]{0:T(1024)(128)(4,1)} %bitcast.64), calls=%async_computation.11 | async-start | bytes 8388608
  124.2 1.6 copy-start.6
  126.1 7.6 %copy-start.7 = (f32[1,5120]{1,0:T(1,128)S(1)}, f32[1,5120]{1,0:T(1,128)}, u32[]{:S(2)}) copy-start(f32[1,5120]{1,0:T(1,128)} %get-tuple-element.24) | copy-start | bytes 61444
  139.8 113.5 %all-gather.6.cloned.1.call-start = ((), (), s32[]{:S(2)}) async-start(), calls=%async_computation.4 | async-start | bytes 1474560 | tf_op jit(solution)/shard_map/all_gather | solution.py:49
  211.1 135.5 %reduce-scatter.5.cloned.1.call-start = ((), (), s32[]{:S(2)}) async-start(), calls=%async_computation.5 | async-start | bytes 2949120 | tf_op jit(solution)/shard_map/reduce_scatter | solution.py:54
  265.0 10.0 %copy-start.1 = (bf16[5120,128]{0,1:T(8,128)(2,1)S(1)}, bf16[5120,128]{0,1:T(8,128)(2,1)}, u32[]{:S(2)}) copy-start(bf16[5120,128]{0,1:T(8,128)(2,1)} %all-gather.6.cloned.1.call-done) | copy-start | bytes 3932164
  277.0 71.3 %copy-start.3 = (bf16[4,640,128]{2,1,0:T(8,128)(2,1)S(1)}, bf16[4,640,128]{2,1,0:T(8,128)(2,1)}, u32[]{:S(2)}) copy-start(bf16[4,640,128]{2,1,0:T(8,128)(2,1)} %param.3) | copy-start | bytes 1966084
  277.0 113.4 %all-gather.8.cloned.1.call-start = ((), (), s32[]{:S(2)}) async-start(), calls=%async_computation.6 | async-start | bytes 1474560 | tf_op jit(solution)/shard_map/all_gather | solution.py:60
  390.4 2.0 copy-start.2
  394.3 30.2 %copy-start.4 = (f32[640,128]{0,1:T(8,128)S(1)}, f32[640,128]{0,1:T(8,128)}, u32[]{:S(2)}) copy-start(f32[640,128]{0,1:T(8,128)} %reduce-scatter.3.cloned.1.call-done) | copy-start | bytes 983044
  394.3 30.1 %copy-start.5 = (f32[640,128]{0,1:T(8,128)S(1)}, f32[640,128]{0,1:T(8,128)}, u32[]{:S(2)}) copy-start(f32[640,128]{0,1:T(8,128)} %reduce-scatter.5.cloned.1.call-done) | copy-start | bytes 983044
Sparse Core Ops, SparseCore 0:
  9.5 88.3 all-gather.3
  139.9 69.4 reduce-scatter.2
  211.7 41.6 all-gather.5
  277.2 69.4 reduce-scatter.4
  348.7 41.6 all-gather.7
where the time goes:
time: 432 us
  waiting for transfers between devices  302 us (70%)
  matrix products  58.9 us (14%)
  other arithmetic  31.1 us (7%)
  blocking collectives  19 us (4%)
  between operations  13.3 us (3%)
  local copies, waits for them, and re-layouts  7.36 us (2%)
    all_gather x1, waiting for transfers between devices, shards(): weights = lax.all_gather(task_weights, 'dp', axis=1, tiled=True)  79 us
    reduce_scatter x1, waiting for transfers between devices, shards(): lax.psum_scatter((ALPHA * inner + (1.0 - ALPHA) * diag) / total, 'dp', sc...  69.6 us
    reduce_scatter x1, waiting for transfers between devices, shards(): lax.psum_scatter((ALPHA * inner + (1.0 - ALPHA) * squares_all * full) / t...  69.6 us
    dot_general x8, matrix products, dot(): lax.dot_general(left, right, (dims, ((), ())), preferred_element_type=jnp...  58.9 us
    all_gather x1, waiting for transfers between devices, shards(): full_bf = lax.all_gather(residual.astype(bf16), 'dp', axis=0, tiled=True)  42.2 us
    all_gather x1, waiting for transfers between devices, shards(): lax.all_gather(image.astype(bf16), 'dp', axis=0, tiled=True).astype(f32)  41.8 us
    psum x1, blocking collectives, shards(): lax.psum((ALPHA * jnp.sum(projected * projected, axis=0) + (1.0 - ALPHA)...  19 us
    reduce_sum x1, other arithmetic, shards(): squares_all = jnp.sum(squares, axis=0)[:, None]  9.47 us
  transfers between devices with their start and end apart: 5, of which 5 were waited for; matrix products, arithmetic and copies ran while one was open for 2% of the time, Pallas kernels for 0%

commit v1 on v0

--- a/solution.py
+++ b/solution.py
@@ -27,7 +27,12 @@
     total = tasks * tokens * lax.axis_size("dp")
     bf16, f32 = (jnp.bfloat16, jnp.float32)
     flat = activations.reshape(tasks * tokens, width)
-    weights = lax.all_gather(task_weights, "dp", axis=1, tiled=True)
+    ring = [task_weights]
+    for hop in range(7):
+        ring.append(lax.ppermute(ring[-1], "dp", [(dev, (dev + 1) % 8) for dev in range(8)]))
+    weights = jnp.roll(
+        jnp.concatenate(ring[::-1], axis=1), (lax.axis_index("dp") + 1) * ring[0].shape[1], axis=1
+    )
     squares = jnp.sum(jnp.square(activations.astype(f32)), axis=1)
     squares_all = jnp.sum(squares, axis=0)[:, None]
     mean = jnp.mean(weights.astype(f32), axis=0)

time: 432 us -> 488 us (1.13)
  waiting for transfers between devices: 302 us -> 328 us
  local copies, waits for them, and re-layouts: 7.36 us -> 30.5 us
    ppermute x0 -> x7, waiting for transfers between devices: none -> 107 us  [shards(): lax.ppermute(ring[-1], 'dp', [(dev, (dev + 1) % 8) for dev in range(8)])]
    all_gather x1 -> x0, waiting for transfers between devices: 79 us -> none  [shards(): weights = lax.all_gather(task_weights, 'dp', axis=1, tiled=True)]
    unnamed x27 -> x44, local copies, waits for them, and re-layouts: 3.55 us -> 20.2 us
    squeeze x1, local copies, waits for them, and re-layouts: 2.09 us -> 7.62 us  [shards(): weights[task]]
  transfers between devices with their start and end apart: 5 -> 11, of which waited for: 5 -> 11; matrix products, arithmetic and copies ran while one was open for 2% -> 2% of each run, Pallas kernels for 0% -> 0%
where the time goes in v1:
time: 488 us; the launch traced here: 487 us
  waiting for transfers between devices  328 us (67%)
  matrix products  59.3 us (12%)
  other arithmetic  34 us (7%)
  local copies, waits for them, and re-layouts  30.5 us (6%)
  blocking collectives  19 us (4%)
  between operations  13.4 us (3%)
    ppermute x7, waiting for transfers between devices, shards(): lax.ppermute(ring[-1], 'dp', [(dev, (dev + 1) % 8) for dev in range(8)])  107 us
    reduce_scatter x1, waiting for transfers between devices, shards(): lax.psum_scatter((ALPHA * inner + (1.0 - ALPHA) * squares_all * full) / t...  69.7 us
    reduce_scatter x1, waiting for transfers between devices, shards(): lax.psum_scatter((ALPHA * inner + (1.0 - ALPHA) * diag) / total, 'dp', sc...  67.2 us
    dot_general x8, matrix products, dot(): lax.dot_general(left, right, (dims, ((), ())), preferred_element_type=jnp...  59.3 us
    all_gather x1, waiting for transfers between devices, shards(): full_bf = lax.all_gather(residual.astype(bf16), 'dp', axis=0, tiled=True)  42 us
    all_gather x1, waiting for transfers between devices, shards(): lax.all_gather(image.astype(bf16), 'dp', axis=0, tiled=True).astype(f32)  41.9 us
    unnamed x44, local copies, waits for them, and re-layouts  20.2 us
    psum x1, blocking collectives, shards(): lax.psum((ALPHA * jnp.sum(projected * projected, axis=0) + (1.0 - ALPHA)...  19 us
  transfers between devices with their start and end apart: 11, of which 11 were waited for; matrix products, arithmetic and copies ran while one was open for 2% of the time, Pallas kernels for 0%

profile of v1, /device:TPU:0, one launch (start us, length us, event | category | flops | bytes accessed | tf_op | source)
XLA Modules:
  0.0 487.3 jit_solution(8937210065055468111)
XLA Ops:
  7.9 3.0 collective-permute-start
  11.0 17.8 %collective-permute-done = bf16[4,640,128]{1,2,0:T(8,128)(2,1)S(1)} collective-permute-done((bf16[4,640,128]{1,2,0:T(8,128)(2,1)S(1)}, bf16[4,640,128]{1,2,0:T(8,128)(2,1)S(1)}, u32[]{:S(2)}, u32[]{:S(2)}) %collective-permute-start) | collective-permute-done | bytes 655392 | tf_op jit(solution)/shard_map/ppermute | solution.py:32
  28.7 18.6 %collective-permute-done.1 = bf16[4,640,128]{1,2,0:T(8,128)(2,1)S(1)} collective-permute-done((bf16[4,640,128]{1,2,0:T(8,128)(2,1)S(1)}, bf16[4,640,128]{1,2,0:T(8,128)(2,1)S(1)}, u32[]{:S(2)}, u32[]{:S(2)}) %collective-permute-start.1) | collective-permute-done | bytes 655392 | tf_op jit(solution)/shard_map/ppermute | solution.py:32
  47.3 17.7 %collective-permute-done.2 = bf16[4,640,128]{1,2,0:T(8,128)(2,1)S(1)} collective-permute-done((bf16[4,640,128]{1,2,0:T(8,128)(2,1)S(1)}, bf16[4,640,128]{1,2,0:T(8,128)(2,1)S(1)}, u32[]{:S(2)}, u32[]{:S(2)}) %collective-permute-start.2) | collective-permute-done | bytes 655392 | tf_op jit(solution)/shard_map/ppermute | solution.py:32
  65.1 16.9 %collective-permute-done.3 = bf16[4,640,128]{1,2,0:T(8,128)(2,1)S(1)} collective-permute-done((bf16[4,640,128]{1,2,0:T(8,128)(2,1)S(1)}, bf16[4,640,128]{1,2,0:T(8,128)(2,1)S(1)}, u32[]{:S(2)}, u32[]{:S(2)}) %collective-permute-start.3) | collective-permute-done | bytes 655392 | tf_op jit(solution)/shard_map/ppermute | solution.py:32
  82.0 16.1 %collective-permute-done.4 = bf16[4,640,128]{1,2,0:T(8,128)(2,1)} collective-permute-done((bf16[4,640,128]{1,2,0:T(8,128)(2,1)S(1)}, bf16[4,640,128]{1,2,0:T(8,128)(2,1)}, u32[]{:S(2)}, u32[]{:S(2)}) %collective-permute-start.4) | collective-permute-done | bytes 655392 | tf_op jit(solution)/shard_map/ppermute | solution.py:32
  98.1 9.5 %fusion = (f32[5120]{0:T(1024)S(1)}, f32[4,5120]{1,0:T(4,128)S(1)}) fusion(bf16[4,512,5120]{2,1,0:T(8,128)(2,1)} %param.2), kind=kLoop, calls=%fused_computation.1 | loop fusion | flops 41917440 | bytes 21073920 | tf_op jit(solution)/shard_map/reduce_sum | solution.py:37
  107.6 6.0 %collective-permute-done.5 = bf16[4,640,128]{1,2,0:T(8,128)(2,1)} collective-permute-done((bf16[4,640,128]{1,2,0:T(8,128)(2,1)}, bf16[4,640,128]{1,2,0:T(8,128)(2,1)}, u32[]{:S(2)}, u32[]{:S(2)}) %collective-permute-start.5) | collective-permute-done | bytes 655392 | tf_op jit(solution)/shard_map/ppermute | solution.py:32
  114.2 13.9 %collective-permute-done.6 = bf16[4,640,128]{1,2,0:T(8,128)(2,1)S(1)} collective-permute-done((bf16[4,640,128]{1,2,0:T(8,128)(2,1)}, bf16[4,640,128]{1,2,0:T(8,128)(2,1)S(1)}, u32[]{:S(2)}, u32[]{:S(2)}) %collective-permute-start.6) | collective-permute-done | bytes 655392 | tf_op jit(solution)/shard_map/ppermute | solution.py:32
  129.1 2.0 constant_dynamic-update-slice_fusion.14
  131.1 2.0 constant_dynamic-update-slice_fusion.13
  138.8 2.0 constant_dynamic-update-slice_fusion.6
  140.8 2.2 constant_dynamic-update-slice_fusion.5
  147.8 5.0 %convert_reduce_fusion = f32[5120,128]{0,1:T(8,128)S(1)} fusion(bf16[4,10240,128]{1,2,0:T(8,128)(2,1)} %constant_dynamic-update-slice_fusion, s32[]{:T(128)S(6)} %select_n.14), kind=kLoop, calls=%fused_computation.3 | loop fusion | flops 4587520 | bytes 7864324 | tf_op jit(solution)/shard_map/reduce_sum | solution.py:38
  152.8 2.0 reduce-precision_convert_fusion
  154.9 7.6 %dynamic-slice_bitcast_fusion.3 = (bf16[5120,128]{0,1:T(8,128)(2,1)S(1)}, bf16[5120,128]{0,1:T(8,128)(2,1)S(1)}, bf16[5120,128]{0,1:T(8,128)(2,1)S(1)}, bf16[5120,128]{0,1:T(8,128)(2,1)}) fusion(bf16[4,10240,128]{1,2,0:T(8,128)(2,1)} %constant_dynamic-update-slice_fusion, s32[]{:T(128)S(6)} %select_n.14, s32[]{:T(128)S(6)} %add.88, s32[]{:T(128)S(6)} %add.87, ...), kind=kLoop, calls=%fused_computation.63 | loop fusion | bytes 10485776 | tf_op jit(solution)/shard_map/squeeze | solution.py:43
  162.6 5.7 %fusion.30 = f32[512,384]{0,1:T(8,128)} fusion(bf16[4,512,5120]{2,1,0:T(8,128)(2,1)S(1)} %bitcast.57, bf16[5120,128]{0,1:T(8,128)(2,1)} %get-tuple-element.16, bf16[5120,128]{0,1:T(8,128)(2,1)} %get-tuple-element.15, bf16[5120,128]{0,1:T(8,128)(2,1)S(1)} %get-tuple-element.11), kind=kOutput, calls=%fused_computation.65 | convolution fusion | flops 2025062400 | bytes 9961472 | tf_op jit(solution)/shard_map/dot_general | solution.py:10
  168.3 5.2 %fusion.33 = f32[512,384]{0,1:T(8,128)} fusion(bf16[4,512,5120]{2,1,0:T(8,128)(2,1)S(1)} %bitcast.57, bf16[5120,128]{0,1:T(8,128)(2,1)} %get-tuple-element.16, bf16[5120,128]{0,1:T(8,128)(2,1)} %get-tuple-element.15, bf16[5120,128]{0,1:T(8,128)(2,1)} %get-tuple-element.14), kind=kOutput, calls=%fused_computation.66 | convolution fusion | flops 2025062400 | bytes 9961472 | tf_op jit(solution)/shard_map/dot_general | solution.py:10
  173.5 4.2 fusion.36
  177.8 4.1 fusion.39
  184.3 7.5 %convolution_bitcast_fusion.1 = f32[5120,256]{0,1:T(8,128)} fusion(bf16[2048,5120]{1,0:T(8,128)(2,1)S(1)} %bitcast.58, bf16[2048,128]{0,1:T(8,128)(2,1)} %get-tuple-element.20, bf16[2048,128]{0,1:T(8,128)(2,1)S(1)} %get-tuple-element.19), kind=kOutput, calls=%fused_computation.5 | convolution fusion | flops 5370806272 | bytes 27262976 | tf_op jit(solution)/shard_map/dot_general | solution.py:10
  191.8 5.6 %fusion.29 = f32[5120,128]{0,1:T(8,128)} fusion(f32[5120,256]{0,1:T(8,128)} %convolution_bitcast_fusion.1, bf16[5120,128]{0,1:T(8,128)(2,1)} %copy-done.2, bf16[5120,128]{0,1:T(8,128)(2,1)} %copy-done.3, bf16[5120,128]{0,1:T(8,128)(2,1)} %get-tuple-element.14, bf16[5120,128]{0,1:T(8,128)(2,1)S(1)} %get-tuple-element.11, ...), kind=kLoop, calls=%fused_computation.52 | loop fusion | flops 13762560 | bytes 15810560 | tf_op jit(solution)/shard_map/div | solution.py:52
  197.5 67.2 %reduce-scatter.3.cloned.1.call-done = f32[640,128]{0,1:T(8,128)} async-done(((f32[5120,128]{0,1:T(8,128)}), f32[640,128]{0,1:T(8,128)}) %reduce-scatter.3.cloned.1.call-update) | async-done | bytes 327696 | tf_op jit(solution)/shard_map/reduce_scatter | solution.py:51
  266.7 42.0 %all-gather.3.cloned.1.call-done = bf16[5120,128]{0,1:T(8,128)(2,1)} async-done(((bf16[640,128]{0,1:T(8,128)(2,1)}), bf16[5120,128]{0,1:T(8,128)(2,1)}) %all-gather.3.cloned.1.call-update) | async-done | bytes 1310736 | tf_op jit(solution)/shard_map/all_gather | solution.py:54
  308.7 11.4 %reduce-precision_convert_fusion.1 = (bf16[2048,128]{0,1:T(8,128)(2,1)S(1)}, bf16[2048,128]{0,1:T(8,128)(2,1)S(1)}) fusion(bf16[5120,128]{0,1:T(8,128)(2,1)} %all-gather.3.cloned.1.call-done, bf16[2048,5120]{1,0:T(8,128)(2,1)} %bitcast.53), kind=kOutput, calls=%fused_computation.57 | convolution fusion | flops 2685403136 | bytes 23330816 | tf_op jit(solution)/shard_map/dot_general | solution.py:10
  320.1 10.0 %convolution_bitcast_fusion = f32[5120,256]{0,1:T(8,128)S(1)} fusion(bf16[2048,5120]{1,0:T(8,128)(2,1)} %bitcast.54, bf16[2048,128]{0,1:T(8,128)(2,1)S(1)} %get-tuple-element.18, bf16[2048,128]{0,1:T(8,128)(2,1)S(1)} %get-tuple-element.17), kind=kOutput, calls=%fused_computation.4 | convolution fusion | flops 5370806272 | bytes 27262976 | tf_op jit(solution)/shard_map/dot_general | solution.py:10
  330.1 2.0 fusion.22
  332.2 69.7 %reduce-scatter.5.cloned.1.call-done = f32[640,128]{0,1:T(8,128)} async-done(((f32[5120,128]{0,1:T(8,128)}), f32[640,128]{0,1:T(8,128)}) %reduce-scatter.5.cloned.1.call-update) | async-done | bytes 327696 | tf_op jit(solution)/shard_map/reduce_scatter | solution.py:59
  403.9 41.9 %all-gather.5.cloned.1.call-done = bf16[5120,128]{0,1:T(8,128)(2,1)} async-done(((bf16[640,128]{0,1:T(8,128)(2,1)}), bf16[5120,128]{0,1:T(8,128)(2,1)}) %all-gather.5.cloned.1.call-update) | async-done | bytes 1310736 | tf_op jit(solution)/shard_map/all_gather | solution.py:65
  445.7 2.0 fusion.23
  449.6 11.1 %fusion.42 = f32[128]{0:T(128)S(1)} fusion(bf16[5120,128]{0,1:T(8,128)(2,1)S(1)} %get-tuple-element.10, bf16[2048,5120]{1,0:T(8,128)(2,1)} %bitcast.55), kind=kOutput, calls=%fused_computation.69 | convolution fusion | flops 2684878848 | bytes 22282752 | tf_op jit(solution)/shard_map/dot_general | solution.py:10
  460.7 19.0 %psum.7 = f32[128]{0:T(128)S(1)} all-reduce(f32[128]{0:T(128)S(1)} %add_multiply_fusion), channel_id=1, replica_groups=mesh['dp'=8,'mp'=4] {'dp'}, use_global_device_ids=true, to_apply=%region_11.12 | all-reduce | flops 128 | bytes 1024 | tf_op jit(solution)/shard_map/psum | solution.py:75
  (73 shorter events, 22.9 us)
Async XLA Ops:
  6.5 258.2 %reduce-scatter.3.cloned.1.call-start = ((), (), s32[]{:S(2)}) async-start(), calls=%async_computation.2 | async-start | bytes 2949120 | tf_op jit(solution)/shard_map/reduce_scatter | solution.py:51
  7.9 20.8 %collective-permute-start = (bf16[4,640,128]{1,2,0:T(8,128)(2,1)S(1)}, bf16[4,640,128]{1,2,0:T(8,128)(2,1)S(1)}, u32[]{:S(2)}, u32[]{:S(2)}) collective-permute-start(bf16[4,640,128]{1,2,0:T(8,128)(2,1)S(1)} %copy.8), channel_id=1, source_target_pairs={{0,4},{4,8},{8,12},{12,16},{16,20},{20,24},{24,28},{28,0},{1,5},{5... | collective-permute-start | bytes 1966088 | tf_op jit(solution)/shard_map/ppermute | solution.py:32
  28.7 18.6 %collective-permute-start.1 = (bf16[4,640,128]{1,2,0:T(8,128)(2,1)S(1)}, bf16[4,640,128]{1,2,0:T(8,128)(2,1)S(1)}, u32[]{:S(2)}, u32[]{:S(2)}) collective-permute-start(bf16[4,640,128]{1,2,0:T(8,128)(2,1)S(1)} %collective-permute-done), channel_id=1, source_target_pairs={{0,4},{4,8},{8,12},{12,16},{16,20},{20,24},{24,28},{28,0},{1,5},{5... | collective-permute-start | bytes 1966088 | tf_op jit(solution)/shard_map/ppermute | solution.py:32
  47.3 17.7 %collective-permute-start.2 = (bf16[4,640,128]{1,2,0:T(8,128)(2,1)S(1)}, bf16[4,640,128]{1,2,0:T(8,128)(2,1)S(1)}, u32[]{:S(2)}, u32[]{:S(2)}) collective-permute-start(bf16[4,640,128]{1,2,0:T(8,128)(2,1)S(1)} %collective-permute-done.1), channel_id=1, source_target_pairs={{0,4},{4,8},{8,12},{12,16},{16,20},{20,24},{24,28},{28,0},{1,5},{5... | collective-permute-start | bytes 1966088 | tf_op jit(solution)/shard_map/ppermute | solution.py:32
  65.1 16.9 %collective-permute-start.3 = (bf16[4,640,128]{1,2,0:T(8,128)(2,1)S(1)}, bf16[4,640,128]{1,2,0:T(8,128)(2,1)S(1)}, u32[]{:S(2)}, u32[]{:S(2)}) collective-permute-start(bf16[4,640,128]{1,2,0:T(8,128)(2,1)S(1)} %collective-permute-done.2), channel_id=1, source_target_pairs={{0,4},{4,8},{8,12},{12,16},{16,20},{20,24},{24,28},{28,0},{1,5},{5... | collective-permute-start | bytes 1966088 | tf_op jit(solution)/shard_map/ppermute | solution.py:32
  82.0 16.1 %collective-permute-start.4 = (bf16[4,640,128]{1,2,0:T(8,128)(2,1)S(1)}, bf16[4,640,128]{1,2,0:T(8,128)(2,1)}, u32[]{:S(2)}, u32[]{:S(2)}) collective-permute-start(bf16[4,640,128]{1,2,0:T(8,128)(2,1)S(1)} %collective-permute-done.3), channel_id=1, source_target_pairs={{0,4},{4,8},{8,12},{12,16},{16,20},{20,24},{24,28},{28,0},{1,5},{5... | collective-permute-start | bytes 1966088 | tf_op jit(solution)/shard_map/ppermute | solution.py:32
  98.1 15.5 %collective-permute-start.5 = (bf16[4,640,128]{1,2,0:T(8,128)(2,1)}, bf16[4,640,128]{1,2,0:T(8,128)(2,1)}, u32[]{:S(2)}, u32[]{:S(2)}) collective-permute-start(bf16[4,640,128]{1,2,0:T(8,128)(2,1)} %collective-permute-done.4), channel_id=1, source_target_pairs={{0,4},{4,8},{8,12},{12,16},{16,20},{20,24},{24,28},{28,0},{1,5},{5... | collective-permute-start | bytes 1966088 | tf_op jit(solution)/shard_map/ppermute | solution.py:32
  113.6 14.5 %collective-permute-start.6 = (bf16[4,640,128]{1,2,0:T(8,128)(2,1)}, bf16[4,640,128]{1,2,0:T(8,128)(2,1)S(1)}, u32[]{:S(2)}, u32[]{:S(2)}) collective-permute-start(bf16[4,640,128]{1,2,0:T(8,128)(2,1)} %collective-permute-done.5), channel_id=1, source_target_pairs={{0,4},{4,8},{8,12},{12,16},{16,20},{20,24},{24,28},{28,0},{1,5},{5... | collective-permute-start | bytes 1966088 | tf_op jit(solution)/shard_map/ppermute | solution.py:32
  135.0 27.5 %slice-start = ((s8[20971520]{0:T(1024)(128)(4,1)}), s8[4194304]{0:T(1024)(128)(4,1)S(1)}, s32[]{:S(2)}) async-start(s8[20971520]{0:T(1024)(128)(4,1)} %bitcast.56), calls=%async_computation.6 | async-start | bytes 8388608
  140.8 21.7 %slice-start.1 = ((s8[20971520]{0:T(1024)(128)(4,1)}), s8[4194304]{0:T(1024)(128)(4,1)S(1)}, s32[]{:S(2)}) async-start(s8[20971520]{0:T(1024)(128)(4,1)} %bitcast.56), calls=%async_computation.7 | async-start | bytes 8388608
  147.8 14.7 %slice-start.2 = ((s8[20971520]{0:T(1024)(128)(4,1)}), s8[4194304]{0:T(1024)(128)(4,1)S(1)}, s32[]{:S(2)}) async-start(s8[20971520]{0:T(1024)(128)(4,1)} %bitcast.56), calls=%async_computation.8 | async-start | bytes 8388608
  152.8 9.7 %slice-start.3 = ((s8[20971520]{0:T(1024)(128)(4,1)}), s8[4194304]{0:T(1024)(128)(4,1)S(1)}, s32[]{:S(2)}) async-start(s8[20971520]{0:T(1024)(128)(4,1)} %bitcast.56), calls=%async_computation.9 | async-start | bytes 8388608
  154.9 7.7 %slice-start.4 = ((s8[20971520]{0:T(1024)(128)(4,1)}), s8[4194304]{0:T(1024)(128)(4,1)S(1)}, s32[]{:S(2)}) async-start(s8[20971520]{0:T(1024)(128)(4,1)} %bitcast.56), calls=%async_computation.10 | async-start | bytes 8388608
  162.5 11.0 %copy-start.3 = (bf16[5120,128]{0,1:T(8,128)(2,1)}, bf16[5120,128]{0,1:T(8,128)(2,1)S(1)}, u32[]{:S(2)}) copy-start(bf16[5120,128]{0,1:T(8,128)(2,1)S(1)} %get-tuple-element.13) | copy-start | bytes 3932164
  162.5 15.2 %copy-start.2 = (bf16[5120,128]{0,1:T(8,128)(2,1)}, bf16[5120,128]{0,1:T(8,128)(2,1)S(1)}, u32[]{:S(2)}) copy-start(bf16[5120,128]{0,1:T(8,128)(2,1)S(1)} %get-tuple-element.12) | copy-start | bytes 3932164
  177.7 4.1 copy-start.7
  184.3 7.5 %copy-start.8 = (f32[1,5120]{1,0:T(1,128)S(1)}, f32[1,5120]{1,0:T(1,128)}, u32[]{:S(2)}) copy-start(f32[1,5120]{1,0:T(1,128)} %get-tuple-element.24) | copy-start | bytes 61444
  197.4 111.2 %all-gather.3.cloned.1.call-start = ((), (), s32[]{:S(2)}) async-start(), calls=%async_computation.3 | async-start | bytes 1474560 | tf_op jit(solution)/shard_map/all_gather | solution.py:54
  266.4 135.5 %reduce-scatter.5.cloned.1.call-start = ((), (), s32[]{:S(2)}) async-start(), calls=%async_computation.4 | async-start | bytes 2949120 | tf_op jit(solution)/shard_map/reduce_scatter | solution.py:59
  320.1 10.0 %copy-start = (bf16[5120,128]{0,1:T(8,128)(2,1)S(1)}, bf16[5120,128]{0,1:T(8,128)(2,1)}, u32[]{:S(2)}) copy-start(bf16[5120,128]{0,1:T(8,128)(2,1)} %all-gather.3.cloned.1.call-done) | copy-start | bytes 3932164
  332.2 71.5 %copy-start.4 = (bf16[4,640,128]{2,1,0:T(8,128)(2,1)S(1)}, bf16[4,640,128]{2,1,0:T(8,128)(2,1)}, u32[]{:S(2)}) copy-start(bf16[4,640,128]{2,1,0:T(8,128)(2,1)} %param.3) | copy-start | bytes 1966084
  332.2 113.5 %all-gather.5.cloned.1.call-start = ((), (), s32[]{:S(2)}) async-start(), calls=%async_computation.5 | async-start | bytes 1474560 | tf_op jit(solution)/shard_map/all_gather | solution.py:65
  445.7 2.0 copy-start.1
  449.6 30.2 %copy-start.5 = (f32[640,128]{0,1:T(8,128)S(1)}, f32[640,128]{0,1:T(8,128)}, u32[]{:S(2)}) copy-start(f32[640,128]{0,1:T(8,128)} %reduce-scatter.3.cloned.1.call-done) | copy-start | bytes 983044
  449.6 30.2 %copy-start.6 = (f32[640,128]{0,1:T(8,128)S(1)}, f32[640,128]{0,1:T(8,128)}, u32[]{:S(2)}) copy-start(f32[640,128]{0,1:T(8,128)} %reduce-scatter.5.cloned.1.call-done) | copy-start | bytes 983044
Sparse Core Ops, SparseCore 0:
  197.6 67.1 reduce-scatter.2
  266.9 41.6 all-gather.2
  332.3 69.5 reduce-scatter.4
  404.0 41.6 all-gather.4
